TPU v7x, 128 devices: a whole 4x4x4 slice. The times are simulated.
128 devices in a mesh: occ: 8 (over y, core), vir: 16 (over z, x).
Axes of the slice: x: 4, y: 4, z: 4, core: 2. Of those that a mesh axis runs over, the one named last changes fastest.
Arguments:
- amplitudes: bfloat16 [9216, 16384], P('occ', 'vir'), may hold values from -6 to 6
- integrals: bfloat16 [16, 8, 1024, 1024], P('vir'), may hold values from -0.0625 to 0.0625
- cd_tiles: int32 [16, 8], P('vir'), may hold values from 0 to 15, as said below
- cd_count: int32 [16], P('vir'), may hold values from 1 to 8, as said below
Outputs:
- residual: bfloat16 [9216, 16384], P('occ', 'vir')
Inputs may be any that keep to these rules, and one draw needn't show every extreme that they name: `cd_tiles`: entries of one row are distinct and the first is the row's own pair tile. `cd_count`: slots at or past the count are unused.
All inputs are finite; a program needn't handle non-finite values.
Results may differ from a plain program's by a relative error of at most 0.0075.
Values may be sent and summed in bfloat16 or wider, within the bound.
No kernel may reach another device: no remote copies, remote signals or barrier semaphores. Data moves between devices by JAX's collectives and lax.ppermute only.
A program may use at most 128 MiB of HBM per device.

v0:
```python
import jax
import jax.numpy as jnp
from jax import lax
from jax.sharding import PartitionSpec as P

TW = 32
K = 1024
OCC_DEV = 12
CD_MAX = 8


def swapped(shard, axis, apart):
    return lax.ppermute(shard, axis, [(i, i ^ 1 << apart) for i in range(lax.axis_size(axis))])


def reflect_rows(matrix):
    occ_devices = lax.axis_size("occ")
    reshaped = matrix.reshape(OCC_DEV, occ_devices, OCC_DEV, matrix.shape[1])
    arrived = lax.all_to_all(reshaped, "occ", split_axis=1, concat_axis=1, tiled=True)
    return arrived.transpose(2, 1, 0, 3).reshape(matrix.shape)


def reflect_tiles(matrix):
    arrived = swapped(matrix, "vir", 0)
    row_count = matrix.shape[0]
    return arrived.reshape(row_count, TW, TW).transpose(0, 2, 1).reshape(row_count, K)


def on_device(amplitudes, integrals, cd_tiles, cd_count):
    row_count = amplitudes.shape[0]
    listed = cd_tiles[0]
    live_count = cd_count[0]
    blocks = integrals[0]
    zero_block = jnp.zeros((row_count, K), jnp.float32)

    def product(col_tile, slot_index):
        int_block = lax.dynamic_index_in_dim(blocks, slot_index, 0, keepdims=False)
        return lax.dot_general(
            col_tile, int_block, (((1,), (1,)), ((), ())), preferred_element_type=jnp.float32
        )

    gathered = lax.all_gather(amplitudes, "vir", axis=1, tiled=True)

    def visit_slot(slot_pos, running):
        tile_id = listed[slot_pos]

        def apply_block(current):
            col_tile = lax.dynamic_slice_in_dim(gathered, tile_id * K, K, 1)
            return current + product(col_tile, slot_pos)

        return lax.cond(slot_pos < live_count, apply_block, lambda current: current, running)

    ladder = lax.fori_loop(0, CD_MAX, visit_slot, zero_block)
    ladder = ladder.astype(jnp.bfloat16)
    mirrored = reflect_tiles(reflect_rows(ladder))
    summed = ladder.astype(jnp.float32) + mirrored.astype(jnp.float32)
    return summed.astype(jnp.bfloat16)


def solution(mesh):
    placed = (P("occ", "vir"), P("vir", None, None, None), P("vir", None), P("vir"))
    return jax.shard_map(
        on_device, mesh=mesh, in_specs=placed, out_specs=P("occ", "vir"), check_vma=False
    )
```

profile of v0, /device:TPU:6, one launch (start us, length us, event | category | flops | bytes accessed | tf_op | source)
XLA Modules:
  0.0 456.2 jit_solution(4664653060656685572)
XLA Ops:
  6.5 0.0 copy-start
  6.5 0.0 all-gather.2.cloned.1.call-start
  6.5 0.7 all-gather.2.cloned.1.call-update
  7.3 223.1 %all-gather.2.cloned.1.call-done = bf16[1152,16384]{1,0:T(8,128)(2,1)} async-done(((bf16[1152,1024]{1,0:T(8,128)(2,1)}), bf16[1152,16384]{1,0:T(8,128)(2,1)}) %all-gather.2.cloned.1.call-update) | async-done | bytes 37748752 | tf_op jit(solution)/shard_map/all_gather | solution.py:42
  230.4 2.8 broadcast_in_dim.3
  233.1 0.0 copy-done
  233.1 83.6 %while.16 = (s32[]{:T(128)}, f32[1152,1024]{1,0:T(8,128)}, s32[]{:T(128)}, s32[8]{0:T(128)S(1)}, bf16[1152,16384]{1,0:T(8,128)(2,1)}, /*index=5*/bf16[8,1024,1024]{2,1,0:T(8,128)(2,1)}, s32[]{:T(128)}) while((s32[]{:T(128)}, f32[1152,1024]{1,0:T(8,128)}, s32[]{:T(128)}, s32[8]{0:T(128)S(1)}, bf16[1152,16384]{1,0:T(8,128)(2,1)}, ...), condition=%wide.region_3.4_spmd, body=%wide.region_0.3_spmd.sunk | while | flops 2417098752 | bytes 13893871 | solution.py:53
  233.8 9.8 %conditional.2 = (f32[1152,1024]{1,0:T(8,128)}) conditional(s32[]{:T(128)} %convert_element_type.41, f32[1152,1024]{1,0:T(8,128)} %get-tuple-element.236, (s32[]{:T(128)}, s32[8]{0:T(128)S(1)}, bf16[1152,16384]{1,0:T(8,128)(2,1)}, bf16[8,1024,1024]{2,1,0:T(8,128)(2,1)}, f32[1152,1024]{1,0:T(8,128)}) %tuple.45), branch_computations={%region_1.0_spmd, %region_2.2_spmd} | conditional | flops 2417098752 | bytes 13893740 | solution.py:51
  233.8 0.6 dynamic_slice.18
  235.1 8.5 %convolution_add_fusion = f32[1152,1024]{1,0:T(8,128)} fusion(f32[1152,1024]{1,0:T(8,128)} %get-tuple-element.165, bf16[1152,16384]{1,0:T(8,128)(2,1)} %get-tuple-element.166, s32[]{:T(128)S(6)} %select_n.19, bf16[8,1024,1024]{2,1,0:T(8,128)(2,1)} %get-tuple-element.169, s32[]{:T(128)S(6)} %select_n.18), kind=kOutput, calls=%fused_computation | convolution fusion | flops 2417098752 | bytes 13893640 | tf_op jit(solution)/shard_map/while/body/eval_jaxpr/cond/branch_1_fun/dot_general | solution.py:38
  244.2 9.8 %conditional.2 = (f32[1152,1024]{1,0:T(8,128)}) conditional(s32[]{:T(128)} %convert_element_type.41, f32[1152,1024]{1,0:T(8,128)} %get-tuple-element.236, (s32[]{:T(128)}, s32[8]{0:T(128)S(1)}, bf16[1152,16384]{1,0:T(8,128)(2,1)}, bf16[8,1024,1024]{2,1,0:T(8,128)(2,1)}, f32[1152,1024]{1,0:T(8,128)}) %tuple.45), branch_computations={%region_1.0_spmd, %region_2.2_spmd} | conditional | flops 2417098752 | bytes 13893740 | solution.py:51
  244.3 0.6 dynamic_slice.18
  245.5 8.5 %convolution_add_fusion = f32[1152,1024]{1,0:T(8,128)} fusion(f32[1152,1024]{1,0:T(8,128)} %get-tuple-element.165, bf16[1152,16384]{1,0:T(8,128)(2,1)} %get-tuple-element.166, s32[]{:T(128)S(6)} %select_n.19, bf16[8,1024,1024]{2,1,0:T(8,128)(2,1)} %get-tuple-element.169, s32[]{:T(128)S(6)} %select_n.18), kind=kOutput, calls=%fused_computation | convolution fusion | flops 2417098752 | bytes 13893640 | tf_op jit(solution)/shard_map/while/body/eval_jaxpr/cond/branch_1_fun/dot_general | solution.py:38
  254.7 9.8 %conditional.2 = (f32[1152,1024]{1,0:T(8,128)}) conditional(s32[]{:T(128)} %convert_element_type.41, f32[1152,1024]{1,0:T(8,128)} %get-tuple-element.236, (s32[]{:T(128)}, s32[8]{0:T(128)S(1)}, bf16[1152,16384]{1,0:T(8,128)(2,1)}, bf16[8,1024,1024]{2,1,0:T(8,128)(2,1)}, f32[1152,1024]{1,0:T(8,128)}) %tuple.45), branch_computations={%region_1.0_spmd, %region_2.2_spmd} | conditional | flops 2417098752 | bytes 13893740 | solution.py:51
  254.7 0.6 dynamic_slice.18
  256.0 8.5 %convolution_add_fusion = f32[1152,1024]{1,0:T(8,128)} fusion(f32[1152,1024]{1,0:T(8,128)} %get-tuple-element.165, bf16[1152,16384]{1,0:T(8,128)(2,1)} %get-tuple-element.166, s32[]{:T(128)S(6)} %select_n.19, bf16[8,1024,1024]{2,1,0:T(8,128)(2,1)} %get-tuple-element.169, s32[]{:T(128)S(6)} %select_n.18), kind=kOutput, calls=%fused_computation | convolution fusion | flops 2417098752 | bytes 13893640 | tf_op jit(solution)/shard_map/while/body/eval_jaxpr/cond/branch_1_fun/dot_general | solution.py:38
  265.1 9.8 %conditional.2 = (f32[1152,1024]{1,0:T(8,128)}) conditional(s32[]{:T(128)} %convert_element_type.41, f32[1152,1024]{1,0:T(8,128)} %get-tuple-element.236, (s32[]{:T(128)}, s32[8]{0:T(128)S(1)}, bf16[1152,16384]{1,0:T(8,128)(2,1)}, bf16[8,1024,1024]{2,1,0:T(8,128)(2,1)}, f32[1152,1024]{1,0:T(8,128)}) %tuple.45), branch_computations={%region_1.0_spmd, %region_2.2_spmd} | conditional | flops 2417098752 | bytes 13893740 | solution.py:51
  265.2 0.6 dynamic_slice.18
  266.4 8.5 %convolution_add_fusion = f32[1152,1024]{1,0:T(8,128)} fusion(f32[1152,1024]{1,0:T(8,128)} %get-tuple-element.165, bf16[1152,16384]{1,0:T(8,128)(2,1)} %get-tuple-element.166, s32[]{:T(128)S(6)} %select_n.19, bf16[8,1024,1024]{2,1,0:T(8,128)(2,1)} %get-tuple-element.169, s32[]{:T(128)S(6)} %select_n.18), kind=kOutput, calls=%fused_computation | convolution fusion | flops 2417098752 | bytes 13893640 | tf_op jit(solution)/shard_map/while/body/eval_jaxpr/cond/branch_1_fun/dot_general | solution.py:38
  275.6 9.8 %conditional.2 = (f32[1152,1024]{1,0:T(8,128)}) conditional(s32[]{:T(128)} %convert_element_type.41, f32[1152,1024]{1,0:T(8,128)} %get-tuple-element.236, (s32[]{:T(128)}, s32[8]{0:T(128)S(1)}, bf16[1152,16384]{1,0:T(8,128)(2,1)}, bf16[8,1024,1024]{2,1,0:T(8,128)(2,1)}, f32[1152,1024]{1,0:T(8,128)}) %tuple.45), branch_computations={%region_1.0_spmd, %region_2.2_spmd} | conditional | flops 2417098752 | bytes 13893740 | solution.py:51
  275.6 0.6 dynamic_slice.18
  276.8 8.5 %convolution_add_fusion = f32[1152,1024]{1,0:T(8,128)} fusion(f32[1152,1024]{1,0:T(8,128)} %get-tuple-element.165, bf16[1152,16384]{1,0:T(8,128)(2,1)} %get-tuple-element.166, s32[]{:T(128)S(6)} %select_n.19, bf16[8,1024,1024]{2,1,0:T(8,128)(2,1)} %get-tuple-element.169, s32[]{:T(128)S(6)} %select_n.18), kind=kOutput, calls=%fused_computation | convolution fusion | flops 2417098752 | bytes 13893640 | tf_op jit(solution)/shard_map/while/body/eval_jaxpr/cond/branch_1_fun/dot_general | solution.py:38
  286.0 9.8 %conditional.2 = (f32[1152,1024]{1,0:T(8,128)}) conditional(s32[]{:T(128)} %convert_element_type.41, f32[1152,1024]{1,0:T(8,128)} %get-tuple-element.236, (s32[]{:T(128)}, s32[8]{0:T(128)S(1)}, bf16[1152,16384]{1,0:T(8,128)(2,1)}, bf16[8,1024,1024]{2,1,0:T(8,128)(2,1)}, f32[1152,1024]{1,0:T(8,128)}) %tuple.45), branch_computations={%region_1.0_spmd, %region_2.2_spmd} | conditional | flops 2417098752 | bytes 13893740 | solution.py:51
  286.0 0.6 dynamic_slice.18
  287.3 8.5 %convolution_add_fusion = f32[1152,1024]{1,0:T(8,128)} fusion(f32[1152,1024]{1,0:T(8,128)} %get-tuple-element.165, bf16[1152,16384]{1,0:T(8,128)(2,1)} %get-tuple-element.166, s32[]{:T(128)S(6)} %select_n.19, bf16[8,1024,1024]{2,1,0:T(8,128)(2,1)} %get-tuple-element.169, s32[]{:T(128)S(6)} %select_n.18), kind=kOutput, calls=%fused_computation | convolution fusion | flops 2417098752 | bytes 13893640 | tf_op jit(solution)/shard_map/while/body/eval_jaxpr/cond/branch_1_fun/dot_general | solution.py:38
  296.5 9.8 %conditional.2 = (f32[1152,1024]{1,0:T(8,128)}) conditional(s32[]{:T(128)} %convert_element_type.41, f32[1152,1024]{1,0:T(8,128)} %get-tuple-element.236, (s32[]{:T(128)}, s32[8]{0:T(128)S(1)}, bf16[1152,16384]{1,0:T(8,128)(2,1)}, bf16[8,1024,1024]{2,1,0:T(8,128)(2,1)}, f32[1152,1024]{1,0:T(8,128)}) %tuple.45), branch_computations={%region_1.0_spmd, %region_2.2_spmd} | conditional | flops 2417098752 | bytes 13893740 | solution.py:51
  296.5 0.6 dynamic_slice.18
  297.7 8.5 %convolution_add_fusion = f32[1152,1024]{1,0:T(8,128)} fusion(f32[1152,1024]{1,0:T(8,128)} %get-tuple-element.165, bf16[1152,16384]{1,0:T(8,128)(2,1)} %get-tuple-element.166, s32[]{:T(128)S(6)} %select_n.19, bf16[8,1024,1024]{2,1,0:T(8,128)(2,1)} %get-tuple-element.169, s32[]{:T(128)S(6)} %select_n.18), kind=kOutput, calls=%fused_computation | convolution fusion | flops 2417098752 | bytes 13893640 | tf_op jit(solution)/shard_map/while/body/eval_jaxpr/cond/branch_1_fun/dot_general | solution.py:38
  306.9 9.8 %conditional.2 = (f32[1152,1024]{1,0:T(8,128)}) conditional(s32[]{:T(128)} %convert_element_type.41, f32[1152,1024]{1,0:T(8,128)} %get-tuple-element.236, (s32[]{:T(128)}, s32[8]{0:T(128)S(1)}, bf16[1152,16384]{1,0:T(8,128)(2,1)}, bf16[8,1024,1024]{2,1,0:T(8,128)(2,1)}, f32[1152,1024]{1,0:T(8,128)}) %tuple.45), branch_computations={%region_1.0_spmd, %region_2.2_spmd} | conditional | flops 2417098752 | bytes 13893740 | solution.py:51
  306.9 0.6 dynamic_slice.18
  308.2 8.5 %convolution_add_fusion = f32[1152,1024]{1,0:T(8,128)} fusion(f32[1152,1024]{1,0:T(8,128)} %get-tuple-element.165, bf16[1152,16384]{1,0:T(8,128)(2,1)} %get-tuple-element.166, s32[]{:T(128)S(6)} %select_n.19, bf16[8,1024,1024]{2,1,0:T(8,128)(2,1)} %get-tuple-element.169, s32[]{:T(128)S(6)} %select_n.18), kind=kOutput, calls=%fused_computation | convolution fusion | flops 2417098752 | bytes 13893640 | tf_op jit(solution)/shard_map/while/body/eval_jaxpr/cond/branch_1_fun/dot_general | solution.py:38
  316.7 3.6 copy.11
  320.3 2.5 copy.12
  322.8 4.8 %reshape.14 = bf16[12,8,12,1024]{3,2,1,0:T(8,128)(2,1)} reshape(bf16[1152,1024]{1,0:T(8,128)(2,1)} %copy.12) | data formatting | bytes 4718592 | tf_op jit(solution)/shard_map/reshape | solution.py:18
  327.6 2.4 copy.13
  330.1 42.5 %all_to_all.5 = bf16[12,8,12,1024]{3,2,0,1:T(8,128)(2,1)S(1)} all-to-all(bf16[12,8,12,1024]{3,2,0,1:T(8,128)(2,1)S(1)} %copy.13), channel_id=1, replica_groups=mesh['occ'=8,'vir'=16] {'occ'}, dimensions={1} | all-to-all | bytes 4718592 | tf_op jit(solution)/shard_map/all_to_all | solution.py:19
  372.6 3.0 copy.14
  375.6 4.9 %reshape.15 = bf16[1152,1024]{1,0:T(8,128)(2,1)} reshape(bf16[12,8,12,1024]{3,2,1,0:T(8,128)(2,1)} %copy.14) | data formatting | bytes 4718592 | tf_op jit(solution)/shard_map/reshape | solution.py:20
  380.5 0.0 collective-permute-start
  380.5 52.9 %collective-permute-done = bf16[1152,1024]{1,0:T(8,128)(2,1)} collective-permute-done((bf16[1152,1024]{1,0:T(8,128)(2,1)}, bf16[1152,1024]{1,0:T(8,128)(2,1)}, u32[]{:S(2)}, u32[]{:S(2)}) %collective-permute-start) | collective-permute-done | bytes 2359328 | tf_op jit(solution)/shard_map/ppermute | solution.py:13
  433.4 4.6 copy.15
  438.0 5.1 %copy.16 = f32[1152,32,32]{0,2,1:T(8,128)S(1)} copy(f32[1152,32,32]{0,1,2:T(8,128)} %bitcast.15) | data formatting | bytes 9437184 | tf_op jit(solution)/shard_map/convert_element_type | solution.py:56
  443.1 2.0 fusion.4
  445.1 4.3 copy.17
Async XLA Ops:
  6.5 226.6 %copy-start = (s32[1,8]{1,0:T(1,128)S(1)}, s32[1,8]{1,0:T(1,128)}, u32[]{:S(2)}) copy-start(s32[1,8]{1,0:T(1,128)} %param.10) | copy-start | bytes 100
  6.5 223.8 %all-gather.2.cloned.1.call-start = ((), (), s32[]{:S(2)}) async-start(), calls=%async_computation.1 | async-start | bytes 40108032 | tf_op jit(solution)/shard_map/all_gather | solution.py:42
  380.5 52.9 %collective-permute-start = (bf16[1152,1024]{1,0:T(8,128)(2,1)}, bf16[1152,1024]{1,0:T(8,128)(2,1)}, u32[]{:S(2)}, u32[]{:S(2)}) collective-permute-start(bf16[1152,1024]{1,0:T(8,128)(2,1)} %reshape.15), channel_id=1, source_target_pairs={{0,1},{1,0},{2,3},{3,2},{4,5},{5,4},{6,7},{7,6},{8,9},{9,8},{10,11... | collective-permute-start | bytes 7077896 | tf_op jit(solution)/shard_map/ppermute | solution.py:13
Sparse Core Ops, SparseCore 0:
  9.5 220.8 all-gather.1
where the time goes:
time: 457 us; the launch traced here: 456 us
  waiting for transfers between devices  277 us (61%)
  matrix products  68.2 us (15%)
  local copies, waits for them, and re-layouts  42.8 us (9%)
  blocking collectives  42.5 us (9%)
  between operations  13.4 us (3%)
  loops' own time  10.5 us (2%)
    all_gather x1, waiting for transfers between devices, on_device(): gathered = lax.all_gather(amplitudes, 'vir', axis=1, tiled=True)  223 us
    dot_general x8, matrix products, product(): lax.dot_general(col_tile, int_block, (((1,), (1,)), ((), ())), preferred_...  68.2 us
    ppermute x1, waiting for transfers between devices, swapped(): lax.ppermute(shard, axis, [(i, i ^ 1 << apart) for i in range(lax.axis_si...  52.9 us
    all_to_all x1, blocking collectives, reflect_rows(): lax.all_to_all(reshaped, 'occ', split_axis=1, concat_axis=1, tiled=True)  42.5 us
    convert_element_type x2, local copies, waits for them, and re-layouts, on_device(): summed = ladder.astype(jnp.float32) + mirrored.astype(jnp.float32)  9.62 us
  transfers between devices with their start and end apart: 2, of which 2 were waited for; matrix products, arithmetic and copies ran while one was open for 0% of the time, Pallas kernels for 0%

commit v1 on v0

--- a/solution.py
+++ b/solution.py
@@ -39,7 +39,9 @@
             col_tile, int_block, (((1,), (1,)), ((), ())), preferred_element_type=jnp.float32
         )
 
-    gathered = lax.all_gather(amplitudes, "vir", axis=1, tiled=True)
+    gathered = jnp.concatenate(
+        lax.all_to_all(jnp.stack([amplitudes] * lax.axis_size("vir")), "vir", 0, 0), axis=1
+    )
 
     def visit_slot(slot_pos, running):
         tile_id = listed[slot_pos]

time: 457 us -> 895 us (1.96)
  waiting for transfers between devices: 277 us -> 608 us
  local copies, waits for them, and re-layouts: 42.8 us -> 148 us
  between operations: 13.4 us -> 0.03 us
    all_to_all x0 -> x1, waiting for transfers between devices: none -> 555 us  [on_device(): lax.all_to_all(jnp.stack([amplitudes] * lax.axis_size('vir')), 'vir', 0, 0)]
    all_gather x1 -> x0, waiting for transfers between devices: 223 us -> none  [on_device(): gathered = lax.all_gather(amplitudes, 'vir', axis=1, tiled=True)]
    while x1 -> x2, local copies, waits for them, and re-layouts: 3.58 us -> 51.3 us  [on_device(): ladder = lax.fori_loop(0, CD_MAX, visit_slot, zero_block)]
    all_to_all x0 -> x1, local copies, waits for them, and re-layouts: none -> 43.7 us  [on_device(): lax.all_to_all(jnp.stack([amplitudes] * lax.axis_size('vir')), 'vir', 0, 0)]
    another operation x0 -> x1, local copies, waits for them, and re-layouts: none -> 13.6 us  [on_device(): jnp.stack([amplitudes] * lax.axis_size('vir'))]
where the time goes in v1:
time: 895 us; the launch traced here: 888 us
  waiting for transfers between devices  608 us (68%)
  local copies, waits for them, and re-layouts  148 us (17%)
  matrix products  68 us (8%)
  blocking collectives  42.7 us (5%)
  loops' own time  10.5 us (1%)
    all_to_all x1, waiting for transfers between devices, on_device(): lax.all_to_all(jnp.stack([amplitudes] * lax.axis_size('vir')), 'vir', 0, 0)  555 us
    dot_general x8, matrix products, product(): lax.dot_general(col_tile, int_block, (((1,), (1,)), ((), ())), preferred_...  68 us
    ppermute x1, waiting for transfers between devices, swapped(): lax.ppermute(shard, axis, [(i, i ^ 1 << apart) for i in range(lax.axis_si...  52.9 us
    while x2, local copies, waits for them, and re-layouts, on_device(): ladder = lax.fori_loop(0, CD_MAX, visit_slot, zero_block)  51.3 us
    all_to_all x1, local copies, waits for them, and re-layouts, on_device(): lax.all_to_all(jnp.stack([amplitudes] * lax.axis_size('vir')), 'vir', 0, 0)  43.7 us
    all_to_all x1, blocking collectives, reflect_rows(): lax.all_to_all(reshaped, 'occ', split_axis=1, concat_axis=1, tiled=True)  42.7 us
  transfers between devices with their start and end apart: 2, of which 2 were waited for; matrix products, arithmetic and copies ran while one was open for 0% of the time, Pallas kernels for 0%

profile of v1, /device:TPU:6, one launch (start us, length us, event | category | flops | bytes accessed | tf_op | source)
XLA Modules:
  0.0 887.9 jit_solution(4209219337471703904)
XLA Ops:
  0.0 13.6 %stack.2 = bf16[16,1152,1024]{2,1,0:T(8,128)(2,1)} broadcast(bf16[1152,1024]{1,0:T(8,128)(2,1)} %param.8), dimensions={1,2} | broadcast | bytes 40108032 | tf_op jit(solution)/shard_map/stack | solution.py:43
  13.6 8.3 all-to-all-start
  21.9 555.4 %all-to-all-done = bf16[16,1152,1024]{2,1,0:T(8,128)(2,1)} async-done(((bf16[16,1152,1024]{2,1,0:T(8,128)(2,1)}), bf16[16,1152,1024]{2,1,0:T(8,128)(2,1)}, u32[]{:S(2)}, u32[]{:S(2)}) %all-to-all-start) | async-done | bytes 37748768 | tf_op jit(solution)/shard_map/all_to_all | solution.py:43
  577.3 43.7 %copy.18 = bf16[16,1152,1024]{1,2,0:T(8,128)(2,1)} copy(bf16[16,1152,1024]{2,1,0:T(8,128)(2,1)} %all-to-all-done) | data formatting | bytes 75497472 | tf_op jit(solution)/shard_map/all_to_all | solution.py:43
  620.9 47.7 %copy.19 = bf16[1152,16384]{1,0:T(8,128)(2,1)} copy(bf16[1152,16384]{0,1:T(8,128)(2,1)} %bitcast.18) | data formatting | bytes 75497472 | tf_op jit(solution)/shard_map/while | solution.py:55
  668.6 0.0 copy-start
  668.6 2.7 broadcast_in_dim.3
  671.4 0.0 copy-done
  671.4 83.7 %while.16 = (s32[]{:T(128)}, f32[1152,1024]{1,0:T(8,128)}, s32[]{:T(128)}, s32[8]{0:T(128)S(1)}, bf16[1152,16384]{1,0:T(8,128)(2,1)}, /*index=5*/bf16[8,1024,1024]{2,1,0:T(8,128)(2,1)}, s32[]{:T(128)}) while((s32[]{:T(128)}, f32[1152,1024]{1,0:T(8,128)}, s32[]{:T(128)}, s32[8]{0:T(128)S(1)}, bf16[1152,16384]{1,0:T(8,128)(2,1)}, ...), condition=%wide.region_3.4_spmd, body=%wide.region_0.3_spmd.sunk | while | flops 2417098752 | bytes 13893871 | solution.py:55
  672.0 9.8 %conditional.2 = (f32[1152,1024]{1,0:T(8,128)}) conditional(s32[]{:T(128)} %convert_element_type.41, f32[1152,1024]{1,0:T(8,128)} %get-tuple-element.242, (s32[]{:T(128)}, s32[8]{0:T(128)S(1)}, bf16[1152,16384]{1,0:T(8,128)(2,1)}, bf16[8,1024,1024]{2,1,0:T(8,128)(2,1)}, f32[1152,1024]{1,0:T(8,128)}) %tuple.46), branch_computations={%region_1.0_spmd, %region_2.2_spmd} | conditional | flops 2417098752 | bytes 13893740 | solution.py:53
  672.1 0.6 dynamic_slice.18
  673.3 8.5 convolution_add_fusion
  682.5 9.8 %conditional.2 = (f32[1152,1024]{1,0:T(8,128)}) conditional(s32[]{:T(128)} %convert_element_type.41, f32[1152,1024]{1,0:T(8,128)} %get-tuple-element.242, (s32[]{:T(128)}, s32[8]{0:T(128)S(1)}, bf16[1152,16384]{1,0:T(8,128)(2,1)}, bf16[8,1024,1024]{2,1,0:T(8,128)(2,1)}, f32[1152,1024]{1,0:T(8,128)}) %tuple.46), branch_computations={%region_1.0_spmd, %region_2.2_spmd} | conditional | flops 2417098752 | bytes 13893740 | solution.py:53
  682.5 0.6 dynamic_slice.18
  683.8 8.5 convolution_add_fusion
  693.0 9.8 %conditional.2 = (f32[1152,1024]{1,0:T(8,128)}) conditional(s32[]{:T(128)} %convert_element_type.41, f32[1152,1024]{1,0:T(8,128)} %get-tuple-element.242, (s32[]{:T(128)}, s32[8]{0:T(128)S(1)}, bf16[1152,16384]{1,0:T(8,128)(2,1)}, bf16[8,1024,1024]{2,1,0:T(8,128)(2,1)}, f32[1152,1024]{1,0:T(8,128)}) %tuple.46), branch_computations={%region_1.0_spmd, %region_2.2_spmd} | conditional | flops 2417098752 | bytes 13893740 | solution.py:53
  693.0 0.6 dynamic_slice.18
  694.2 8.5 convolution_add_fusion
  703.4 9.8 %conditional.2 = (f32[1152,1024]{1,0:T(8,128)}) conditional(s32[]{:T(128)} %convert_element_type.41, f32[1152,1024]{1,0:T(8,128)} %get-tuple-element.242, (s32[]{:T(128)}, s32[8]{0:T(128)S(1)}, bf16[1152,16384]{1,0:T(8,128)(2,1)}, bf16[8,1024,1024]{2,1,0:T(8,128)(2,1)}, f32[1152,1024]{1,0:T(8,128)}) %tuple.46), branch_computations={%region_1.0_spmd, %region_2.2_spmd} | conditional | flops 2417098752 | bytes 13893740 | solution.py:53
  703.4 0.6 dynamic_slice.18
  704.7 8.5 convolution_add_fusion
  713.9 9.8 %conditional.2 = (f32[1152,1024]{1,0:T(8,128)}) conditional(s32[]{:T(128)} %convert_element_type.41, f32[1152,1024]{1,0:T(8,128)} %get-tuple-element.242, (s32[]{:T(128)}, s32[8]{0:T(128)S(1)}, bf16[1152,16384]{1,0:T(8,128)(2,1)}, bf16[8,1024,1024]{2,1,0:T(8,128)(2,1)}, f32[1152,1024]{1,0:T(8,128)}) %tuple.46), branch_computations={%region_1.0_spmd, %region_2.2_spmd} | conditional | flops 2417098752 | bytes 13893740 | solution.py:53
  713.9 0.6 dynamic_slice.18
  715.2 8.5 convolution_add_fusion
  724.3 9.8 %conditional.2 = (f32[1152,1024]{1,0:T(8,128)}) conditional(s32[]{:T(128)} %convert_element_type.41, f32[1152,1024]{1,0:T(8,128)} %get-tuple-element.242, (s32[]{:T(128)}, s32[8]{0:T(128)S(1)}, bf16[1152,16384]{1,0:T(8,128)(2,1)}, bf16[8,1024,1024]{2,1,0:T(8,128)(2,1)}, f32[1152,1024]{1,0:T(8,128)}) %tuple.46), branch_computations={%region_1.0_spmd, %region_2.2_spmd} | conditional | flops 2417098752 | bytes 13893740 | solution.py:53
  724.4 0.6 dynamic_slice.18
  725.6 8.5 convolution_add_fusion
  734.8 9.8 %conditional.2 = (f32[1152,1024]{1,0:T(8,128)}) conditional(s32[]{:T(128)} %convert_element_type.41, f32[1152,1024]{1,0:T(8,128)} %get-tuple-element.242, (s32[]{:T(128)}, s32[8]{0:T(128)S(1)}, bf16[1152,16384]{1,0:T(8,128)(2,1)}, bf16[8,1024,1024]{2,1,0:T(8,128)(2,1)}, f32[1152,1024]{1,0:T(8,128)}) %tuple.46), branch_computations={%region_1.0_spmd, %region_2.2_spmd} | conditional | flops 2417098752 | bytes 13893740 | solution.py:53
  734.8 0.6 dynamic_slice.18
  736.1 8.5 convolution_add_fusion
  745.2 9.8 %conditional.2 = (f32[1152,1024]{1,0:T(8,128)}) conditional(s32[]{:T(128)} %convert_element_type.41, f32[1152,1024]{1,0:T(8,128)} %get-tuple-element.242, (s32[]{:T(128)}, s32[8]{0:T(128)S(1)}, bf16[1152,16384]{1,0:T(8,128)(2,1)}, bf16[8,1024,1024]{2,1,0:T(8,128)(2,1)}, f32[1152,1024]{1,0:T(8,128)}) %tuple.46), branch_computations={%region_1.0_spmd, %region_2.2_spmd} | conditional | flops 2417098752 | bytes 13893740 | solution.py:53
  745.3 0.6 dynamic_slice.18
  746.5 8.5 convolution_add_fusion
  755.1 3.6 copy.20
  758.6 2.5 copy.21
  761.1 4.8 reshape.24
  766.0 2.4 copy.22
  768.4 42.7 %all_to_all.10 = bf16[12,8,12,1024]{3,2,0,1:T(8,128)(2,1)S(1)} all-to-all(bf16[12,8,12,1024]{3,2,0,1:T(8,128)(2,1)S(1)} %copy.22), channel_id=1, replica_groups=mesh['occ'=8,'vir'=16] {'occ'}, dimensions={1} | all-to-all | bytes 4718592 | tf_op jit(solution)/shard_map/all_to_all | solution.py:19
  811.2 3.0 copy.23
  814.1 4.9 reshape.25
  819.1 0.0 collective-permute-start
  819.1 52.9 %collective-permute-done = bf16[1152,1024]{1,0:T(8,128)(2,1)} collective-permute-done((bf16[1152,1024]{1,0:T(8,128)(2,1)}, bf16[1152,1024]{1,0:T(8,128)(2,1)}, u32[]{:S(2)}, u32[]{:S(2)}) %collective-permute-start) | collective-permute-done | bytes 2359328 | tf_op jit(solution)/shard_map/ppermute | solution.py:13
  872.0 4.6 copy.24
  876.6 5.1 copy.25
  881.7 2.0 fusion.4
  883.6 4.3 copy.26
Async XLA Ops:
  13.6 563.7 %all-to-all-start = ((bf16[16,1152,1024]{2,1,0:T(8,128)(2,1)}), bf16[16,1152,1024]{2,1,0:T(8,128)(2,1)}, u32[]{:S(2)}, u32[]{:S(2)}) async-start(bf16[16,1152,1024]{2,1,0:T(8,128)(2,1)} %stack.2), calls=%async_computation | async-start | bytes 75497472 | tf_op jit(solution)/shard_map/all_to_all | solution.py:43
  668.6 2.7 copy-start
  819.1 52.9 %collective-permute-start = (bf16[1152,1024]{1,0:T(8,128)(2,1)}, bf16[1152,1024]{1,0:T(8,128)(2,1)}, u32[]{:S(2)}, u32[]{:S(2)}) collective-permute-start(bf16[1152,1024]{1,0:T(8,128)(2,1)} %reshape.25), channel_id=1, source_target_pairs={{0,1},{1,0},{2,3},{3,2},{4,5},{5,4},{6,7},{7,6},{8,9},{9,8},{10,11... | collective-permute-start | bytes 7077896 | tf_op jit(solution)/shard_map/ppermute | solution.py:13
